TPU v7x, 32 devices: a whole 2x2x4 slice. The times are simulated.
32 devices in a mesh: mem: 8 (over z, y), job: 4 (over x, core).
Axes of the slice: x: 2, y: 2, z: 4, core: 2. Of those that a mesh axis runs over, the one named last changes fastest.
Arguments:
- pair_cost: bfloat16 [1536, 128, 128], P(('mem', 'job')), may hold values from -6 to 6
- pair_coef: bfloat16 [1536, 128, 128], P(('mem', 'job')), may hold values from 0.049804688 to 0.5
- slot_member: int32 [32, 48], P(('mem', 'job')), may hold values from 0 to 31, never falling along the last dimension, each value on 1 to 4 neighbouring positions
- slot_owner: int32 [32, 48, 1], P(('mem', 'job')), may hold values from 0 to 7; in each aligned block of 48 rows (0 to 47, 48 to 95, ..., all dimensions but the last counted through in order) at most 9 rows name the same one
- slot_local: int32 [32, 48], P(('mem', 'job')), may hold values from 0 to 15
- duals: float32 [512, 128], P(('mem', 'job')), may hold values from 0.1 to 3
- capacity: int32 [512, 128], P(('mem', 'job')), may hold values from 0 to 39
Outputs:
- primal: bfloat16 [1536, 128, 128], P(('mem', 'job'))
- gradient: float32 [512, 128], P(('mem', 'job'))
- member_share: float32 [256, 128], P('mem')
Inputs may be any that keep to these rules, and one draw needn't show every extreme that they name: `slot_member`: in each device's row the values never fall, every value appears, none more than 4 times, and one exactly 4 times. `slot_owner`: among the 48 entries of one device no value appears more than 9 times, and in some devices one appears exactly 9 times.
All inputs are finite; a program needn't handle non-finite values.
Results may differ from a plain program's by a relative error of at most 0.001.
Values sent between devices are 32-bit elements; how exact they have to be, the bound alone decides.
A program may use at most 64 MiB of HBM per device.

v0:
```python
import jax
import jax.numpy as jnp
from jax import lax
from jax.sharding import PartitionSpec as P

MB_DEV = 32
RIDGE = 1.0


def allocate(pair_cost, pair_coef, dual_rows):
    reduced = pair_cost.astype(jnp.float32) + pair_coef.astype(jnp.float32) * dual_rows[:, None, :]
    allocation = jnp.clip(-reduced / RIDGE, 0.0, 1.0)
    column_part = jnp.sum(pair_coef.astype(jnp.float32) * allocation, axis=1)
    row_part = jnp.sum(allocation, axis=2)
    return (allocation.astype(jnp.bfloat16), column_part, row_part)


def per_device(pair_cost, pair_coef, slot_member, slot_owner, slot_local, duals, capacity):
    slot_count = pair_cost.shape[0]
    block_size = pair_cost.shape[1]
    job_blocks = duals.shape[0]
    mem_count = lax.axis_size("mem")
    owner_index = slot_owner[0, :, 0]
    local_index = slot_local[0]
    peer_slots = max(2, (3 * slot_count + 2 * mem_count - 1) // (2 * mem_count))
    owner_table = (owner_index[:, None] == jnp.arange(mem_count, dtype=jnp.int32)[None, :]).astype(
        jnp.int32
    )
    slot_rank = jnp.sum((jnp.cumsum(owner_table, axis=0) - owner_table) * owner_table, axis=1)
    position = owner_index * peer_slots + slot_rank
    requests = jnp.zeros((mem_count * peer_slots,), jnp.int32).at[position].set(local_index)
    requests = requests.reshape(mem_count, peer_slots)
    received = lax.all_to_all(requests, "mem", split_axis=0, concat_axis=0, tiled=True)
    replies = duals[received]
    fetched, received = (
        lax.all_to_all(replies, "mem", split_axis=0, concat_axis=0, tiled=True),
        received,
    )
    dual_rows = fetched.reshape(mem_count * peer_slots, block_size)[position]
    primal, column_part, row_part = allocate(pair_cost, pair_coef, dual_rows)
    outgoing = (
        jnp.zeros((mem_count * peer_slots, block_size), jnp.float32).at[position].set(column_part)
    )
    incoming = lax.all_to_all(
        outgoing.reshape(mem_count, peer_slots, block_size),
        "mem",
        split_axis=0,
        concat_axis=0,
        tiled=True,
    )
    totals = jax.ops.segment_sum(
        incoming.reshape(mem_count * peer_slots, block_size),
        received.reshape(-1),
        num_segments=job_blocks,
    )
    gradient = totals - capacity.astype(jnp.float32)
    member_table = (jnp.arange(MB_DEV, dtype=jnp.int32)[:, None] == slot_member[0][None, :]).astype(
        jnp.float32
    )
    member_part = jnp.dot(
        member_table, row_part, precision=lax.Precision.HIGHEST, preferred_element_type=jnp.float32
    )
    member_share = lax.psum(member_part, "job") / block_size
    return (primal, gradient, member_share)


def solution(mesh):
    placed = (
        P(("mem", "job"), None, None),
        P(("mem", "job"), None, None),
        P(("mem", "job"), None),
        P(("mem", "job"), None, None),
        P(("mem", "job"), None),
        P(("mem", "job"), None),
        P(("mem", "job"), None),
    )
    return jax.shard_map(
        per_device,
        mesh=mesh,
        in_specs=placed,
        out_specs=(P(("mem", "job"), None, None), P(("mem", "job"), None), P("mem", None)),
        check_vma=False,
    )
```

profile of v0, /device:TPU:0, one launch (start us, length us, event | category | flops | bytes accessed | tf_op | source)
XLA Modules:
  0.0 57.0 jit_solution(11159333356886695551)
XLA Ops:
  0.6 0.0 copy-start
  0.6 0.7 %fusion.6 = s32[48,8]{1,0:T(8,128)S(1)} fusion(s32[48]{0:T(128)} %bitcast.20), kind=kLoop, calls=%fused_computation.15 | loop fusion | flops 768 | bytes 1728 | tf_op jit(solution)/shard_map/convert_element_type | solution.py:26
  1.4 0.1 reduce_window_sum.11
  1.5 0.8 %select_reduce_fusion = s32[48]{0:T(128)S(1)} fusion(s32[48,8]{1,0:T(8,128)S(1)} %reduce_window_sum.11, s32[48]{0:T(128)} %bitcast.21), kind=kLoop, calls=%fused_computation.13 | loop fusion | flops 1872 | bytes 1920 | tf_op jit(solution)/shard_map/reduce_sum | solution.py:29
  2.3 0.7 %fusion.13 = s32[48]{0:T(128)S(1)} fusion(s32[48]{0:T(128)S(1)} %select_reduce_fusion, s32[1,48,1]{1,2,0:T(1,128)} %param.10), kind=kLoop, calls=%fused_computation.29 | loop fusion | flops 240 | bytes 576 | tf_op jit(solution)/shard_map/select_n | solution.py:31
  3.0 0.9 %scatter_custom_fusion = s32[72]{0:T(128)S(1)} fusion(s32[48]{0:T(128)S(1)} %fusion.13, s32[48]{0:T(128)} %bitcast.23, s32[]{:T(128)} %constant.8.clone.1), kind=kCustom, calls=%fused_computation.31 | custom fusion | bytes 800 | tf_op jit(solution)/shard_map/scatter | solution.py:31
  3.8 0.1 all_to_all.14
  3.9 13.6 %all_to_all.22 = s32[8,1,9]{2,1,0:T(1,128)S(1)} all-to-all(s32[8,1,9]{2,1,0:T(1,128)S(1)} %bitcast.19), channel_id=1, replica_groups=mesh['mem'=8,'job'=4] {'mem'}, dimensions={0} | all-to-all | bytes 576 | tf_op jit(solution)/shard_map/all_to_all | solution.py:33
  17.5 0.1 reshape.83
  17.6 0.0 copy-done
  17.6 0.6 %gather_fusion = f32[72,128]{1,0:T(8,128)S(1)} fusion(f32[16,128]{1,0:T(8,128)S(1)} %copy-done, s32[1024]{0:T(1024)S(1)} %pad_clamp_fusion.1), kind=kCustom, calls=%fused_computation | custom fusion | bytes 74016 | tf_op jit(solution)/shard_map/gather | solution.py:34
  18.2 0.6 %reshape.82 = f32[8,9,128]{2,1,0:T(8,128)} reshape(f32[72,128]{1,0:T(8,128)S(1)} %gather_fusion) | data formatting | bytes 73728 | tf_op jit(solution)/shard_map/gather | solution.py:34
  18.8 3.4 %all-to-all-start.1 = ((f32[8,9,128]{2,1,0:T(8,128)}), f32[8,9,128]{2,1,0:T(8,128)S(1)}, u32[]{:S(2)}, u32[]{:S(2)}) async-start(f32[8,9,128]{2,1,0:T(8,128)} %reshape.82), calls=%async_computation.1 | async-start | bytes 131072 | tf_op jit(solution)/shard_map/all_to_all | solution.py:36
  22.2 0.5 broadcast.65
  22.7 0.7 %reduce.3 = s32[8,9]{1,0:T(8,128)S(1)} reduce(s32[8,1,9]{2,1,0:T(1,128)S(1)} %all_to_all.22, s32[]{:T(128)} %broadcast.65), dimensions={1}, to_apply=%all_to_all.15.reduce_sub_computation.3 | reduce | bytes 580 | tf_op jit(solution)/shard_map/all_to_all | solution.py:33
  23.4 0.1 reshape.115
  23.5 5.6 %all-to-all-done.1 = f32[8,9,128]{2,1,0:T(8,128)S(1)} async-done(((f32[8,9,128]{2,1,0:T(8,128)}), f32[8,9,128]{2,1,0:T(8,128)S(1)}, u32[]{:S(2)}, u32[]{:S(2)}) %all-to-all-start.1) | async-done | bytes 36896 | tf_op jit(solution)/shard_map/all_to_all | solution.py:36
  29.0 0.6 %gather_fusion.1 = f32[48,128]{1,0:T(8,128)S(1)} fusion(f32[72,128]{1,0:T(8,128)S(1)} %reshape.78, s32[1024]{0:T(1024)S(1)} %pad_clamp_fusion), kind=kCustom, calls=%fused_computation.1 | custom fusion | bytes 49344 | tf_op jit(solution)/shard_map/gather | solution.py:39
  29.6 0.0 copy-start.2
  29.6 0.0 copy-start.1
  29.6 4.1 %fusion.4 = (f32[48,128]{1,0:T(8,128)S(1)}, f32[48,128]{1,0:T(8,128)S(1)}, bf16[48,128,128]{2,1,0:T(8,128)(2,1)}) fusion(bf16[48,128,128]{2,1,0:T(8,128)(2,1)} %param.8, bf16[48,128,128]{2,1,0:T(8,128)(2,1)} %param.7, f32[48,128]{1,0:T(8,128)S(1)} %gather_fusion.1), kind=kLoop, calls=%fused_computation.11 | loop fusion | flops 7852032 | bytes 4792320 | tf_op jit(solution)/shard_map/reduce_sum | solution.py:14
  33.8 0.0 copy-done.2
  33.8 0.1 fusion.9
  33.9 10.1 %psum.7 = f32[32,128]{1,0:T(8,128)S(1)} all-reduce(f32[32,128]{1,0:T(8,128)S(1)} %fusion.9), channel_id=1, replica_groups=mesh['mem'=8,'job'=4] {'job'}, use_global_device_ids=true, to_apply=%region_7.8 | all-reduce | flops 4096 | bytes 32768 | tf_op jit(solution)/shard_map/psum | solution.py:63
  44.0 0.7 %scatter_custom_fusion.1 = f32[72,128]{1,0:T(8,128)S(1)} fusion(s32[48]{0:T(128)S(1)} %fusion.13, f32[48,128]{1,0:T(8,128)S(1)} %get-tuple-element.4, f32[]{:T(128)} %constant.7.clone.1), kind=kCustom, calls=%fused_computation.16 | custom fusion | bytes 36868 | tf_op jit(solution)/shard_map/scatter | solution.py:42
  44.7 0.6 %reshape.79 = f32[8,9,128]{2,1,0:T(8,128)} reshape(f32[72,128]{1,0:T(8,128)S(1)} %scatter_custom_fusion.1) | data formatting | bytes 73728 | tf_op jit(solution)/shard_map/reshape | solution.py:45
  45.3 3.3 %all-to-all-start.2 = ((f32[8,9,128]{2,1,0:T(8,128)}), f32[8,9,128]{2,1,0:T(8,128)S(1)}, u32[]{:S(2)}, u32[]{:S(2)}) async-start(f32[8,9,128]{2,1,0:T(8,128)} %reshape.79), calls=%async_computation.2 | async-start | bytes 131072 | tf_op jit(solution)/shard_map/all_to_all | solution.py:44
  48.7 0.6 %broadcast_multiply_fusion = f32[32,128]{1,0:T(8,128)} fusion(f32[32,128]{1,0:T(8,128)S(1)} %psum.7), kind=kLoop, calls=%fused_computation.21 | loop fusion | flops 4096 | bytes 32768 | tf_op jit(solution)/shard_map/div | solution.py:63
  49.3 6.2 %all-to-all-done.2 = f32[8,9,128]{2,1,0:T(8,128)S(1)} async-done(((f32[8,9,128]{2,1,0:T(8,128)}), f32[8,9,128]{2,1,0:T(8,128)S(1)}, u32[]{:S(2)}, u32[]{:S(2)}) %all-to-all-start.2) | async-done | bytes 36896 | tf_op jit(solution)/shard_map/all_to_all | solution.py:44
  55.5 0.8 %scatter_custom_fusion.2 = f32[16,128]{1,0:T(8,128)S(1)} fusion(s32[72]{0:T(128)S(1)} %reshape.115, f32[72,128]{1,0:T(8,128)S(1)} %reshape.117, f32[]{:T(128)} %constant.7.clone.1), kind=kCustom, calls=%fused_computation.26 | custom fusion | flops 9216 | bytes 8196 | tf_op jit(solution)/shard_map/scatter-add | solution.py:51
  56.3 0.0 copy-done.1
  56.3 0.6 %convert_subtract_fusion = f32[16,128]{1,0:T(8,128)} fusion(f32[16,128]{1,0:T(8,128)S(1)} %scatter_custom_fusion.2, s32[16,128]{1,0:T(8,128)S(1)} %copy-done.1), kind=kLoop, calls=%fused_computation.23 | loop fusion | flops 4096 | bytes 24576 | tf_op jit(solution)/shard_map/sub | solution.py:56
  (5 shorter events, 0.0 us)
Async XLA Ops:
  0.6 17.0 %copy-start = (f32[16,128]{1,0:T(8,128)S(1)}, f32[16,128]{1,0:T(8,128)}, u32[]{:S(2)}) copy-start(f32[16,128]{1,0:T(8,128)} %param.12) | copy-start | bytes 24580
  18.8 10.2 %all-to-all-start.1 = ((f32[8,9,128]{2,1,0:T(8,128)}), f32[8,9,128]{2,1,0:T(8,128)S(1)}, u32[]{:S(2)}, u32[]{:S(2)}) async-start(f32[8,9,128]{2,1,0:T(8,128)} %reshape.82), calls=%async_computation.1 | async-start | bytes 131072 | tf_op jit(solution)/shard_map/all_to_all | solution.py:36
  29.6 4.1 %copy-start.2 = (s32[1,48]{1,0:T(1,128)S(1)}, s32[1,48]{1,0:T(1,128)}, u32[]{:S(2)}) copy-start(s32[1,48]{1,0:T(1,128)} %param.9) | copy-start | bytes 580
  29.6 26.7 %copy-start.1 = (s32[16,128]{1,0:T(8,128)S(1)}, s32[16,128]{1,0:T(8,128)}, u32[]{:S(2)}) copy-start(s32[16,128]{1,0:T(8,128)} %param.13) | copy-start | bytes 24580
  45.3 10.2 %all-to-all-start.2 = ((f32[8,9,128]{2,1,0:T(8,128)}), f32[8,9,128]{2,1,0:T(8,128)S(1)}, u32[]{:S(2)}, u32[]{:S(2)}) async-start(f32[8,9,128]{2,1,0:T(8,128)} %reshape.79), calls=%async_computation.2 | async-start | bytes 131072 | tf_op jit(solution)/shard_map/all_to_all | solution.py:44
where the time goes:
time: 57.4 us; the launch traced here: 57 us
  blocking collectives  23.7 us (41%)
  waiting for transfers between devices  11.8 us (21%)
  other arithmetic  9.12 us (16%)
  starting transfers between devices  6.7 us (12%)
  local copies, waits for them, and re-layouts  4.76 us (8%)
  between operations  0.73 us (1%)
    all_to_all x1, blocking collectives, per_device(): lax.all_to_all(requests, 'mem', split_axis=0, concat_axis=0, tiled=True)  13.6 us
    psum x1, blocking collectives, per_device(): member_share = lax.psum(member_part, 'job') / block_size  10.1 us
    all_to_all x1, waiting for transfers between devices, per_device(): lax.all_to_all(outgoing.reshape(mem_count, peer_slots, block_size), 'mem'...  6.23 us
    all_to_all x1, waiting for transfers between devices, per_device(): lax.all_to_all(replies, 'mem', split_axis=0, concat_axis=0, tiled=True)  5.57 us
    reduce_sum x1, other arithmetic, allocate(): row_part = jnp.sum(allocation, axis=2)  4.11 us
    all_to_all x1, starting transfers between devices, per_device(): lax.all_to_all(replies, 'mem', split_axis=0, concat_axis=0, tiled=True)  3.35 us
    all_to_all x1, starting transfers between devices, per_device(): lax.all_to_all(outgoing.reshape(mem_count, peer_slots, block_size), 'mem'...  3.35 us
    gather x2, local copies, waits for them, and re-layouts, per_device(): replies = duals[received]  1.24 us
  transfers between devices with their start and end apart: 2, of which 2 were waited for; matrix products, arithmetic and copies ran while one was open for 3% of the time, Pallas kernels for 0%

commit v1 on v0

--- a/solution.py
+++ b/solution.py
@@ -60,7 +60,7 @@
     member_part = jnp.dot(
         member_table, row_part, precision=lax.Precision.HIGHEST, preferred_element_type=jnp.float32
     )
-    member_share = lax.psum(member_part, "job") / block_size
+    member_share = jnp.sum(lax.all_gather(member_part, "job"), axis=0) / block_size
     return (primal, gradient, member_share)
 
 

time: 57.4 us -> 47.1 us (0.82)
  waiting for transfers between devices: 11.8 us -> 6.42 us
  blocking collectives: 23.7 us -> 18.8 us
    psum x1 -> x0, blocking collectives: 10.1 us -> none  [per_device(): member_share = lax.psum(member_part, 'job') / block_size]
    all_to_all x1, waiting for transfers between devices: 6.23 us -> 0.85 us  [per_device(): lax.all_to_all(outgoing.reshape(mem_count, peer_slots, block_size), 'mem'...]
    all_gather x0 -> x1, blocking collectives: none -> 5.23 us  [per_device(): lax.all_gather(member_part, 'job')]
  transfers between devices with their start and end apart: 2 -> 2, of which waited for: 2 -> 2; matrix products, arithmetic and copies ran while one was open for 3% -> 4% of each run, Pallas kernels for 0% -> 0%
where the time goes in v1:
time: 47.1 us; the launch traced here: 46.7 us
  blocking collectives  18.8 us (40%)
  other arithmetic  9.13 us (19%)
  starting transfers between devices  6.7 us (14%)
  waiting for transfers between devices  6.42 us (14%)
  local copies, waits for them, and re-layouts  4.76 us (10%)
  between operations  0.74 us (2%)
    all_to_all x1, blocking collectives, per_device(): lax.all_to_all(requests, 'mem', split_axis=0, concat_axis=0, tiled=True)  13.6 us
    all_to_all x1, waiting for transfers between devices, per_device(): lax.all_to_all(replies, 'mem', split_axis=0, concat_axis=0, tiled=True)  5.57 us
    all_gather x1, blocking collectives, per_device(): lax.all_gather(member_part, 'job')  5.23 us
    reduce_sum x1, other arithmetic, allocate(): row_part = jnp.sum(allocation, axis=2)  4.11 us
    all_to_all x1, starting transfers between devices, per_device(): lax.all_to_all(replies, 'mem', split_axis=0, concat_axis=0, tiled=True)  3.35 us
    all_to_all x1, starting transfers between devices, per_device(): lax.all_to_all(outgoing.reshape(mem_count, peer_slots, block_size), 'mem'...  3.35 us
    gather x2, local copies, waits for them, and re-layouts, per_device(): replies = duals[received]  1.24 us
  transfers between devices with their start and end apart: 2, of which 2 were waited for; matrix products, arithmetic and copies ran while one was open for 4% of the time, Pallas kernels for 0%

profile of v1, /device:TPU:0, one launch (start us, length us, event | category | flops | bytes accessed | tf_op | source)
XLA Modules:
  0.0 46.7 jit_solution(8303487828590666413)
XLA Ops:
  0.6 0.0 copy-start
  0.6 0.7 %fusion.6 = s32[48,8]{1,0:T(8,128)S(1)} fusion(s32[48]{0:T(128)} %bitcast.22), kind=kLoop, calls=%fused_computation.15 | loop fusion | flops 768 | bytes 1728 | tf_op jit(solution)/shard_map/convert_element_type | solution.py:26
  1.4 0.1 reduce_window_sum.11
  1.5 0.8 %select_reduce_fusion = s32[48]{0:T(128)S(1)} fusion(s32[48,8]{1,0:T(8,128)S(1)} %reduce_window_sum.11, s32[48]{0:T(128)} %bitcast.23), kind=kLoop, calls=%fused_computation.13 | loop fusion | flops 1872 | bytes 1920 | tf_op jit(solution)/shard_map/reduce_sum | solution.py:29
  2.3 0.7 %fusion.13 = s32[48]{0:T(128)S(1)} fusion(s32[48]{0:T(128)S(1)} %select_reduce_fusion, s32[1,48,1]{1,2,0:T(1,128)} %param.10), kind=kLoop, calls=%fused_computation.29 | loop fusion | flops 240 | bytes 576 | tf_op jit(solution)/shard_map/select_n | solution.py:31
  3.0 0.9 %scatter_custom_fusion = s32[72]{0:T(128)S(1)} fusion(s32[48]{0:T(128)S(1)} %fusion.13, s32[48]{0:T(128)} %bitcast.25, s32[]{:T(128)} %constant.8.clone.1), kind=kCustom, calls=%fused_computation.31 | custom fusion | bytes 800 | tf_op jit(solution)/shard_map/scatter | solution.py:31
  3.8 0.1 all_to_all.14
  3.9 13.6 %all_to_all.22 = s32[8,1,9]{2,1,0:T(1,128)S(1)} all-to-all(s32[8,1,9]{2,1,0:T(1,128)S(1)} %bitcast.21), channel_id=1, replica_groups=mesh['mem'=8,'job'=4] {'mem'}, dimensions={0} | all-to-all | bytes 576 | tf_op jit(solution)/shard_map/all_to_all | solution.py:33
  17.5 0.1 reshape.83
  17.6 0.0 copy-done
  17.6 0.6 %gather_fusion = f32[72,128]{1,0:T(8,128)S(1)} fusion(f32[16,128]{1,0:T(8,128)S(1)} %copy-done, s32[1024]{0:T(1024)S(1)} %pad_clamp_fusion.1), kind=kCustom, calls=%fused_computation | custom fusion | bytes 74016 | tf_op jit(solution)/shard_map/gather | solution.py:34
  18.2 0.6 %reshape.82 = f32[8,9,128]{2,1,0:T(8,128)} reshape(f32[72,128]{1,0:T(8,128)S(1)} %gather_fusion) | data formatting | bytes 73728 | tf_op jit(solution)/shard_map/gather | solution.py:34
  18.8 3.4 %all-to-all-start.1 = ((f32[8,9,128]{2,1,0:T(8,128)}), f32[8,9,128]{2,1,0:T(8,128)S(1)}, u32[]{:S(2)}, u32[]{:S(2)}) async-start(f32[8,9,128]{2,1,0:T(8,128)} %reshape.82), calls=%async_computation.1 | async-start | bytes 131072 | tf_op jit(solution)/shard_map/all_to_all | solution.py:36
  22.2 0.5 %broadcast.65 = s32[]{:T(128)} broadcast(s32[]{:T(128)} %constant.8.clone.1), dimensions={} | broadcast | bytes 8 | tf_op jit(solution)/shard_map/all_to_all | solution.py:33
  22.7 0.7 %reduce.3 = s32[8,9]{1,0:T(8,128)S(1)} reduce(s32[8,1,9]{2,1,0:T(1,128)S(1)} %all_to_all.22, s32[]{:T(128)} %broadcast.65), dimensions={1}, to_apply=%all_to_all.15.reduce_sub_computation.3 | reduce | bytes 580 | tf_op jit(solution)/shard_map/all_to_all | solution.py:33
  23.4 0.1 reshape.115
  23.5 5.6 %all-to-all-done.1 = f32[8,9,128]{2,1,0:T(8,128)S(1)} async-done(((f32[8,9,128]{2,1,0:T(8,128)}), f32[8,9,128]{2,1,0:T(8,128)S(1)}, u32[]{:S(2)}, u32[]{:S(2)}) %all-to-all-start.1) | async-done | bytes 36896 | tf_op jit(solution)/shard_map/all_to_all | solution.py:36
  29.0 0.6 %gather_fusion.1 = f32[48,128]{1,0:T(8,128)S(1)} fusion(f32[72,128]{1,0:T(8,128)S(1)} %reshape.78, s32[1024]{0:T(1024)S(1)} %pad_clamp_fusion), kind=kCustom, calls=%fused_computation.1 | custom fusion | bytes 49344 | tf_op jit(solution)/shard_map/gather | solution.py:39
  29.6 0.0 copy-start.2
  29.6 0.0 copy-start.1
  29.6 4.1 %fusion.4 = (f32[48,128]{1,0:T(8,128)S(1)}, f32[48,128]{1,0:T(8,128)S(1)}, bf16[48,128,128]{2,1,0:T(8,128)(2,1)}) fusion(bf16[48,128,128]{2,1,0:T(8,128)(2,1)} %param.8, bf16[48,128,128]{2,1,0:T(8,128)(2,1)} %param.7, f32[48,128]{1,0:T(8,128)S(1)} %gather_fusion.1), kind=kLoop, calls=%fused_computation.11 | loop fusion | flops 7852032 | bytes 4792320 | tf_op jit(solution)/shard_map/reduce_sum | solution.py:14
  33.8 0.7 %scatter_custom_fusion.1 = f32[72,128]{1,0:T(8,128)S(1)} fusion(s32[48]{0:T(128)S(1)} %fusion.13, f32[48,128]{1,0:T(8,128)S(1)} %get-tuple-element.4, f32[]{:T(128)} %constant.7.clone.1), kind=kCustom, calls=%fused_computation.16 | custom fusion | bytes 36868 | tf_op jit(solution)/shard_map/scatter | solution.py:42
  34.4 0.6 %reshape.79 = f32[8,9,128]{2,1,0:T(8,128)} reshape(f32[72,128]{1,0:T(8,128)S(1)} %scatter_custom_fusion.1) | data formatting | bytes 73728 | tf_op jit(solution)/shard_map/reshape | solution.py:45
  35.1 3.3 %all-to-all-start.2 = ((f32[8,9,128]{2,1,0:T(8,128)}), f32[8,9,128]{2,1,0:T(8,128)S(1)}, u32[]{:S(2)}, u32[]{:S(2)}) async-start(f32[8,9,128]{2,1,0:T(8,128)} %reshape.79), calls=%async_computation.2 | async-start | bytes 131072 | tf_op jit(solution)/shard_map/all_to_all | solution.py:44
  38.4 0.0 copy-done.2
  38.4 0.1 fusion.9
  38.6 5.2 %all-gather = f32[128,128]{1,0:T(8,128)S(1)} all-gather(f32[32,128]{1,0:T(8,128)S(1)} %fusion.9), channel_id=2, replica_groups=mesh['mem'=8,'job'=4] {'job'}, dimensions={0}, use_global_device_ids=true | all-gather | bytes 81920 | tf_op jit(solution)/shard_map/all_gather | solution.py:63
  43.8 0.6 %broadcast_multiply_fusion = f32[32,128]{1,0:T(8,128)} fusion(f32[32,128]{1,0:T(8,128)S(1)} %reduce_sum.42), kind=kLoop, calls=%fused_computation.21 | loop fusion | flops 4096 | bytes 32768 | tf_op jit(solution)/shard_map/div | solution.py:63
  44.4 0.8 %all-to-all-done.2 = f32[8,9,128]{2,1,0:T(8,128)S(1)} async-done(((f32[8,9,128]{2,1,0:T(8,128)}), f32[8,9,128]{2,1,0:T(8,128)S(1)}, u32[]{:S(2)}, u32[]{:S(2)}) %all-to-all-start.2) | async-done | bytes 36896 | tf_op jit(solution)/shard_map/all_to_all | solution.py:44
  45.3 0.8 %scatter_custom_fusion.2 = f32[16,128]{1,0:T(8,128)S(1)} fusion(s32[72]{0:T(128)S(1)} %reshape.115, f32[72,128]{1,0:T(8,128)S(1)} %reshape.117, f32[]{:T(128)} %constant.7.clone.1), kind=kCustom, calls=%fused_computation.26 | custom fusion | flops 9216 | bytes 8196 | tf_op jit(solution)/shard_map/scatter-add | solution.py:51
  46.1 0.0 copy-done.1
  46.1 0.6 %convert_subtract_fusion = f32[16,128]{1,0:T(8,128)} fusion(f32[16,128]{1,0:T(8,128)S(1)} %scatter_custom_fusion.2, s32[16,128]{1,0:T(8,128)S(1)} %copy-done.1), kind=kLoop, calls=%fused_computation.23 | loop fusion | flops 4096 | bytes 24576 | tf_op jit(solution)/shard_map/sub | solution.py:56
  (6 shorter events, 0.0 us)
Async XLA Ops:
  0.6 17.0 %copy-start = (f32[16,128]{1,0:T(8,128)S(1)}, f32[16,128]{1,0:T(8,128)}, u32[]{:S(2)}) copy-start(f32[16,128]{1,0:T(8,128)} %param.12) | copy-start | bytes 24580
  18.8 10.2 %all-to-all-start.1 = ((f32[8,9,128]{2,1,0:T(8,128)}), f32[8,9,128]{2,1,0:T(8,128)S(1)}, u32[]{:S(2)}, u32[]{:S(2)}) async-start(f32[8,9,128]{2,1,0:T(8,128)} %reshape.82), calls=%async_computation.1 | async-start | bytes 131072 | tf_op jit(solution)/shard_map/all_to_all | solution.py:36
  29.6 8.8 %copy-start.2 = (s32[1,48]{1,0:T(1,128)S(1)}, s32[1,48]{1,0:T(1,128)}, u32[]{:S(2)}) copy-start(s32[1,48]{1,0:T(1,128)} %param.9) | copy-start | bytes 580
  29.6 16.5 %copy-start.1 = (s32[16,128]{1,0:T(8,128)S(1)}, s32[16,128]{1,0:T(8,128)}, u32[]{:S(2)}) copy-start(s32[16,128]{1,0:T(8,128)} %param.13) | copy-start | bytes 24580
  35.1 10.2 %all-to-all-start.2 = ((f32[8,9,128]{2,1,0:T(8,128)}), f32[8,9,128]{2,1,0:T(8,128)S(1)}, u32[]{:S(2)}, u32[]{:S(2)}) async-start(f32[8,9,128]{2,1,0:T(8,128)} %reshape.79), calls=%async_computation.2 | async-start | bytes 131072 | tf_op jit(solution)/shard_map/all_to_all | solution.py:44
